TPU v7x, 32 devices: a whole 2x2x4 slice. The times are simulated.
32 devices in a mesh: groups: 2 (over y), vocab: 8 (over z, x), mp: 2 (over core).
Axes of the slice: x: 2, y: 2, z: 4, core: 2. Of those that a mesh axis runs over, the one named last changes fastest.
Arguments:
- gate_pre: bfloat16 [32, 14336], P(('groups', 'vocab'), 'mp'), parts along dimension 0, may hold values from -6 to 6
- up_pre: bfloat16 [32, 14336], P(('groups', 'vocab'), 'mp'), parts along dimension 0, may hold values from -6 to 6
- down_weight: bfloat16 [8192, 14336], P('vocab', 'mp'), may hold values from -0.046875 to 0.046875
- residual: bfloat16 [32, 8192], P(('groups', 'vocab', 'mp')), parts along dimension 0, may hold values from -36 to 36
- norm_gain: bfloat16 [8192], replicated, may hold values from 0.5 to 1.5
- head_weight: bfloat16 [8192, 4032], P('mp', 'vocab')
- targets: int32 [32], P(('groups', 'mp')), parts along dimension 0, may hold values from 0 to 4031
Outputs:
- log_likelihood: float32 [32], P(('groups', 'mp')), parts along dimension 0
There are 2 independent parts, one for each index of `groups`. A program takes and returns all parts, laid end to end along the dimension named above; an argument that names none is the same for every part. Nothing has to cross between parts.
All inputs are finite; a program needn't handle non-finite values.
Results may differ from a plain program's by a relative error of at most 0.0003.
The roundings to bfloat16 on the way count: a program that leaves them out, or rounds other values in their place, can miss the bound.
Values may be sent and summed in bfloat16 or wider, within the bound.
No kernel may reach another device: no remote copies, remote signals or barrier semaphores. Data moves between devices by JAX's collectives and lax.ppermute only.
A program may use at most 64 MiB of HBM per device.

v0:
```python
import jax
import jax.numpy as jnp
from jax import lax
from jax.sharding import PartitionSpec as P

EPSILON = 1e-05


def merged_2(value, axis, combine):
    everything = jax.tree.map(lambda part: lax.all_gather(part, axis), value)
    first = jax.tree.map(lambda part: part[0], everything)

    def turn(k, so_far):
        return combine(so_far, jax.tree.map(lambda part: part[k], everything))

    return lax.fori_loop(1, lax.axis_size(axis), turn, first)


def merge_stats(earlier, follows):
    joint_max = jnp.maximum(earlier[0], follows[0])
    joint_sum = earlier[1] * jnp.exp(earlier[0] - joint_max) + follows[1] * jnp.exp(
        follows[0] - joint_max
    )
    return (joint_max, joint_sum, earlier[2] + follows[2])


def body(gate_pre, up_pre, down_weight, residual, norm_gain, head_weight, targets):
    vocab_count = lax.axis_size("vocab")
    model_count = lax.axis_size("mp")
    model_index = lax.axis_index("mp")
    vocab_index = lax.axis_index("vocab")
    gated_units = (jax.nn.silu(gate_pre.astype(jnp.float32)) * up_pre.astype(jnp.float32)).astype(
        jnp.bfloat16
    )
    down_terms = lax.dot_general(
        lax.all_gather(gated_units, "vocab", axis=0, tiled=True),
        down_weight,
        (((1,), (1,)), ((), ())),
        preferred_element_type=jnp.float32,
    )
    own_rows = residual.shape[0]
    block_cols = down_weight.shape[0]
    grouped = down_terms.reshape(vocab_count, model_count, own_rows, block_cols)
    arrived = lax.all_to_all(
        lax.all_to_all(grouped, "vocab", split_axis=0, concat_axis=3, tiled=True),
        "mp",
        split_axis=1,
        concat_axis=0,
        tiled=True,
    )
    update = jnp.sum(arrived, axis=(0, 1))
    stream = (residual.astype(jnp.float32) + update).astype(jnp.bfloat16)
    stream = lax.optimization_barrier(stream)
    widened = stream.astype(jnp.float32)
    mean_square = jnp.mean(widened * widened, axis=1, keepdims=True)
    normed = (
        widened * lax.rsqrt(mean_square + EPSILON) * norm_gain.astype(jnp.float32)[None, :]
    ).astype(jnp.bfloat16)
    half_width = head_weight.shape[0]
    halves = lax.dynamic_slice_in_dim(
        lax.all_gather(normed, ("vocab", "mp"), axis=0, tiled=True),
        model_index * half_width,
        half_width,
        1,
    )
    logit_terms = jnp.dot(halves, head_weight, preferred_element_type=jnp.float32)
    logits = lax.psum_scatter(logit_terms, "mp", scatter_dimension=0, tiled=True)
    local_ids = targets - vocab_index * logits.shape[1]
    columns = lax.broadcasted_iota(jnp.int32, logits.shape, 1)
    chosen = jnp.sum(jnp.where(columns == local_ids[:, None], logits, 0.0), axis=1)
    row_top = jnp.max(logits, axis=1)
    exp_total = jnp.sum(jnp.exp(logits - row_top[:, None]), axis=1)
    merged = merged_2((row_top, exp_total, chosen), "vocab", merge_stats)
    return merged[2] - merged[0] - jnp.log(merged[1])


def solution(mesh):
    return jax.shard_map(
        body,
        mesh=mesh,
        in_specs=(
            P(("groups", "vocab"), "mp"),
            P(("groups", "vocab"), "mp"),
            P("vocab", "mp"),
            P(("groups", "vocab", "mp"), None),
            P(),
            P("mp", "vocab"),
            P(("groups", "mp")),
        ),
        out_specs=P(("groups", "mp")),
        check_vma=False,
    )
```

profile of v0, /device:TPU:0, one launch (start us, length us, event | category | flops | bytes accessed | tf_op | source)
XLA Modules:
  0.0 128.8 jit_solution(11626139243467973319)
XLA Ops:
  6.5 0.9 fusion.12
  7.4 32.5 %all-gather.3 = bf16[8,2,7168]{2,1,0:T(2,128)(2,1)S(1)} all-gather(bf16[1,2,7168]{2,1,0:T(2,128)(2,1)S(1)} %fusion.12), channel_id=1, replica_groups=mesh['groups'=2,'vocab'=8,'mp'=2] {'vocab'}, dimensions={0}, use_global_device_ids=true | all-gather | bytes 258048 | tf_op jit(solution)/shard_map/all_gather | solution.py:36
  39.9 0.1 reshape.39
  40.0 9.1 %fusion.14 = f32[16,1024]{1,0:T(8,128)S(1)} fusion(bf16[16,7168]{1,0:T(8,128)(2,1)S(1)} %reshape.39, bf16[1024,7168]{1,0:T(8,128)(2,1)} %param.11), kind=kOutput, calls=%fused_computation.28 | convolution fusion | flops 234881024 | bytes 14974976 | tf_op jit(solution)/shard_map/dot_general | solution.py:35
  49.1 0.7 reshape.18
  49.7 5.5 %all-to-all-start = ((f32[8,2,1,1024]{3,1,2,0:T(2,128)}), f32[8,2,1,1024]{3,1,2,0:T(2,128)S(1)}, u32[]{:S(2)}, u32[]{:S(2)}) async-start(f32[8,2,1,1024]{3,1,2,0:T(2,128)} %bitcast.4), calls=%async_computation | async-start | bytes 131072 | tf_op jit(solution)/shard_map/all_to_all | solution.py:45
  55.2 0.0 reduce-scatter.2.cloned.1.call-start
  55.3 6.8 %all-to-all-done = f32[8,2,1,1024]{3,1,2,0:T(2,128)S(1)} async-done(((f32[8,2,1,1024]{3,1,2,0:T(2,128)}), f32[8,2,1,1024]{3,1,2,0:T(2,128)S(1)}, u32[]{:S(2)}, u32[]{:S(2)}) %all-to-all-start) | async-done | bytes 65568 | tf_op jit(solution)/shard_map/all_to_all | solution.py:45
  62.2 0.1 copy.10
  62.2 3.8 %all_to_all.27 = f32[1,2,1,8192]{3,2,0,1:T(1,128)S(1)} all-to-all(f32[1,2,1,8192]{3,2,0,1:T(1,128)S(1)} %copy.10), channel_id=1, replica_groups=mesh['groups'=2,'vocab'=8,'mp'=2] {'mp'}, dimensions={1} | all-to-all | bytes 131072 | tf_op jit(solution)/shard_map/all_to_all | solution.py:44
  66.0 0.1 reduce_sum.38
  66.1 0.0 copy-done
  66.2 0.7 multiply_reduce_fusion
  67.5 0.1 convert_bitcast_fusion
  67.6 19.5 %all-gather.4 = bf16[16,1,8192]{2,1,0:T(2,128)(2,1)S(1)} all-gather(bf16[1,1,8192]{2,1,0:T(2,128)(2,1)S(1)} %convert_bitcast_fusion), channel_id=1, replica_groups=mesh['groups'=2,'vocab'=8,'mp'=2] {'vocab','mp'}, dimensions={0}, use_global_device_ids=true | all-gather | bytes 278528 | tf_op jit(solution)/shard_map/all_gather | solution.py:61
  87.0 0.3 constant_dynamic-slice_fusion.3
  87.3 4.0 %fusion.7 = f32[16,504]{1,0:T(8,128)} fusion(bf16[4096,504]{0,1:T(8,128)(2,1)} %param.14, bf16[16,1,4096]{2,1,0:T(2,128)(2,1)S(1)} %constant_dynamic-slice_fusion.3), kind=kOutput, calls=%fused_computation.11 | convolution fusion | flops 66060288 | bytes 4292096 | tf_op jit(solution)/shard_map/dot_general | solution.py:66
  91.3 0.0 reduce-scatter.2.cloned.1.call-update
  91.3 0.0 copy-done.2
  91.4 0.6 dynamic-slice
  92.7 4.2 %reduce-scatter.2.cloned.1.call-done = f32[8,504]{1,0:T(8,128)} async-done(((f32[16,504]{1,0:T(8,128)}), f32[8,504]{1,0:T(8,128)}) %reduce-scatter.2.cloned.1.call-update) | async-done | bytes 16144 | tf_op jit(solution)/shard_map/reduce_scatter | solution.py:67
  96.8 0.8 reduce_max.9
  97.7 0.2 dynamic-update-slice
  97.9 0.9 select_reduce_fusion
  98.9 0.2 dynamic-update-slice.2
  99.1 0.2 dynamic-update-slice.1
  99.3 21.5 %all-reduce.3 = (f32[64]{0:T(128)S(1)}, f32[64]{0:T(128)S(1)}, f32[64]{0:T(128)S(1)}) all-reduce(f32[64]{0:T(128)S(1)} %dynamic-update-slice, f32[64]{0:T(128)S(1)} %dynamic-update-slice.1, f32[64]{0:T(128)S(1)} %dynamic-update-slice.2), channel_id=2, replica_groups=mesh['groups'=2,'vocab'=8,'mp'=2] {'vocab'}, use_global_device_ids=true, to_apply=%add | all-reduce | flops 192 | bytes 1536
  120.9 0.1 reshape.20
  120.9 0.1 reshape.21
  121.0 0.1 reshape.22
  121.1 0.3 while.19
  121.4 0.5 log_subtract_fusion
  (19 shorter events, 0.3 us)
Async XLA Ops:
  6.5 84.8 %copy-start.3 = (u32[32]{0:T(128)S(1)}, u32[32]{0:T(128)}, u32[]{:S(2)}) copy-start(u32[32]{0:T(128)} %constant.71) | copy-start | bytes 388
  6.5 48.8 %copy-start.1 = (bf16[8192]{0:T(1024)(128)(2,1)S(1)}, bf16[8192]{0:T(1024)(128)(2,1)}, u32[]{:S(2)}) copy-start(bf16[8192]{0:T(1024)(128)(2,1)} %param.13) | copy-start | bytes 49156
  6.5 59.6 %copy-start = (bf16[1,8192]{1,0:T(2,128)(2,1)S(1)}, bf16[1,8192]{1,0:T(2,128)(2,1)}, u32[]{:S(2)}) copy-start(bf16[1,8192]{1,0:T(2,128)(2,1)} %param.12) | copy-start | bytes 49156
  6.5 84.8 %copy-start.2 = (s32[8]{0:T(128)S(1)}, s32[8]{0:T(128)}, u32[]{:S(2)}) copy-start(s32[8]{0:T(128)} %param.15) | copy-start | bytes 100
  49.7 12.4 %all-to-all-start = ((f32[8,2,1,1024]{3,1,2,0:T(2,128)}), f32[8,2,1,1024]{3,1,2,0:T(2,128)S(1)}, u32[]{:S(2)}, u32[]{:S(2)}) async-start(f32[8,2,1,1024]{3,1,2,0:T(2,128)} %bitcast.4), calls=%async_computation | async-start | bytes 131072 | tf_op jit(solution)/shard_map/all_to_all | solution.py:45
  55.2 41.6 %reduce-scatter.2.cloned.1.call-start = ((), (), s32[]{:S(2)}) async-start(), calls=%async_computation.3 | async-start | bytes 49152 | tf_op jit(solution)/shard_map/reduce_scatter | solution.py:67
Sparse Core Ops, SparseCore 0:
  91.4 5.3 reduce-scatter.1
where the time goes:
time: 129 us
  blocking collectives  77.3 us (60%)
  between operations  14.9 us (12%)
  matrix products  13 us (10%)
  waiting for transfers between devices  11 us (9%)
  starting transfers between devices  5.54 us (4%)
  other arithmetic  4.22 us (3%)
  local copies, waits for them, and re-layouts  2.68 us (2%)
    all_gather x1, blocking collectives, body(): lax.all_gather(gated_units, 'vocab', axis=0, tiled=True)  32.5 us
    unnamed x1, blocking collectives  21.5 us
    all_gather x1, blocking collectives, body(): lax.all_gather(normed, ('vocab', 'mp'), axis=0, tiled=True)  19.5 us
    dot_general x1, matrix products, body(): lax.dot_general(lax.all_gather(gated_units, 'vocab', axis=0, tiled=True),...  9.05 us
    all_to_all x1, waiting for transfers between devices, body(): lax.all_to_all(grouped, 'vocab', split_axis=0, concat_axis=3, tiled=True)  6.83 us
    all_to_all x1, starting transfers between devices, body(): lax.all_to_all(grouped, 'vocab', split_axis=0, concat_axis=3, tiled=True)  5.51 us
    reduce_scatter x1, waiting for transfers between devices, body(): lax.psum_scatter(logit_terms, 'mp', scatter_dimension=0, tiled=True)  4.19 us
    dot_general x1, matrix products, body(): jnp.dot(halves, head_weight, preferred_element_type=jnp.float32)  3.98 us
  transfers between devices with their start and end apart: 2, of which 2 were waited for; matrix products, arithmetic and copies ran while one was open for 1% of the time, Pallas kernels for 0%

commit v1 on v0

--- a/solution.py
+++ b/solution.py
@@ -41,12 +41,20 @@
     own_rows = residual.shape[0]
     block_cols = down_weight.shape[0]
     grouped = down_terms.reshape(vocab_count, model_count, own_rows, block_cols)
-    arrived = lax.all_to_all(
-        lax.all_to_all(grouped, "vocab", split_axis=0, concat_axis=3, tiled=True),
-        "mp",
-        split_axis=1,
-        concat_axis=0,
-        tiled=True,
+    arrived = jnp.concatenate(
+        lax.all_to_all(
+            jnp.stack(
+                jnp.split(
+                    lax.all_to_all(grouped, "vocab", split_axis=0, concat_axis=3, tiled=True),
+                    lax.axis_size("mp"),
+                    axis=1,
+                )
+            ),
+            "mp",
+            0,
+            0,
+        ),
+        axis=0,
     )
     update = jnp.sum(arrived, axis=(0, 1))
     stream = (residual.astype(jnp.float32) + update).astype(jnp.bfloat16)

time: 129 us -> 129 us (level)
  no operation moved by 1% of the time
where the time goes in v1:
time: 129 us
  blocking collectives  77.3 us (60%)
  between operations  14.9 us (12%)
  matrix products  13 us (10%)
  waiting for transfers between devices  11 us (9%)
  starting transfers between devices  5.54 us (4%)
  other arithmetic  4.28 us (3%)
  local copies, waits for them, and re-layouts  2.66 us (2%)
    all_gather x1, blocking collectives, body(): lax.all_gather(gated_units, 'vocab', axis=0, tiled=True)  32.5 us
    unnamed x1, blocking collectives  21.5 us
    all_gather x1, blocking collectives, body(): lax.all_gather(normed, ('vocab', 'mp'), axis=0, tiled=True)  19.5 us
    dot_general x1, matrix products, body(): lax.dot_general(lax.all_gather(gated_units, 'vocab', axis=0, tiled=True),...  9.05 us
    all_to_all x1, waiting for transfers between devices, body(): lax.all_to_all(grouped, 'vocab', split_axis=0, concat_axis=3, tiled=True)  6.83 us
    all_to_all x1, starting transfers between devices, body(): lax.all_to_all(grouped, 'vocab', split_axis=0, concat_axis=3, tiled=True)  5.51 us
    reduce_scatter x1, waiting for transfers between devices, body(): lax.psum_scatter(logit_terms, 'mp', scatter_dimension=0, tiled=True)  4.19 us
    dot_general x1, matrix products, body(): jnp.dot(halves, head_weight, preferred_element_type=jnp.float32)  3.98 us
  transfers between devices with their start and end apart: 2, of which 2 were waited for; matrix products, arithmetic and copies ran while one was open for 1% of the time, Pallas kernels for 0%

profile of v1, /device:TPU:0, one launch (start us, length us, event | category | flops | bytes accessed | tf_op | source)
XLA Modules:
  0.0 128.8 jit_solution(17891329190113405173)
XLA Ops:
  6.5 0.9 fusion.12
  7.4 32.5 %all-gather.3 = bf16[8,2,7168]{2,1,0:T(2,128)(2,1)S(1)} all-gather(bf16[1,2,7168]{2,1,0:T(2,128)(2,1)S(1)} %fusion.12), channel_id=1, replica_groups=mesh['groups'=2,'vocab'=8,'mp'=2] {'vocab'}, dimensions={0}, use_global_device_ids=true | all-gather | bytes 258048 | tf_op jit(solution)/shard_map/all_gather | solution.py:36
  39.9 0.1 reshape.38
  40.0 9.1 %fusion.14 = f32[16,1024]{1,0:T(8,128)S(1)} fusion(bf16[16,7168]{1,0:T(8,128)(2,1)S(1)} %reshape.38, bf16[1024,7168]{1,0:T(8,128)(2,1)} %param.11), kind=kOutput, calls=%fused_computation.31 | convolution fusion | flops 234881024 | bytes 14974976 | tf_op jit(solution)/shard_map/dot_general | solution.py:35
  49.1 0.7 reshape.17
  49.7 5.5 %all-to-all-start = ((f32[8,2,1,1024]{3,1,2,0:T(2,128)}), f32[8,2,1,1024]{3,1,2,0:T(2,128)S(1)}, u32[]{:S(2)}, u32[]{:S(2)}) async-start(f32[8,2,1,1024]{3,1,2,0:T(2,128)} %bitcast.4), calls=%async_computation | async-start | bytes 131072 | tf_op jit(solution)/shard_map/all_to_all | solution.py:48
  55.2 0.0 reduce-scatter.2.cloned.1.call-start
  55.3 0.0 copy-done.1
  55.3 6.8 %all-to-all-done = f32[8,2,1,1024]{3,1,2,0:T(2,128)S(1)} async-done(((f32[8,2,1,1024]{3,1,2,0:T(2,128)}), f32[8,2,1,1024]{3,1,2,0:T(2,128)S(1)}, u32[]{:S(2)}, u32[]{:S(2)}) %all-to-all-start) | async-done | bytes 65568 | tf_op jit(solution)/shard_map/all_to_all | solution.py:48
  62.2 0.1 slice_bitcast_fusion.1
  62.2 0.1 pad_maximum_fusion
  62.3 3.8 %all_to_all.23 = f32[2,1,1,1,8192]{4,3,2,1,0:T(1,128)S(1)} all-to-all(f32[2,1,1,1,8192]{4,3,2,1,0:T(1,128)S(1)} %pad_maximum_fusion), channel_id=1, replica_groups=mesh['groups'=2,'vocab'=8,'mp'=2] {'mp'}, dimensions={0} | all-to-all | bytes 131072 | tf_op jit(solution)/shard_map/all_to_all | solution.py:45
  66.1 0.1 reduce_sum.38
  66.2 0.7 multiply_reduce_fusion
  67.6 0.1 convert_bitcast_fusion
  67.6 19.5 %all-gather.4 = bf16[16,1,8192]{2,1,0:T(2,128)(2,1)S(1)} all-gather(bf16[1,1,8192]{2,1,0:T(2,128)(2,1)S(1)} %convert_bitcast_fusion), channel_id=1, replica_groups=mesh['groups'=2,'vocab'=8,'mp'=2] {'vocab','mp'}, dimensions={0}, use_global_device_ids=true | all-gather | bytes 278528 | tf_op jit(solution)/shard_map/all_gather | solution.py:69
  87.1 0.3 constant_dynamic-slice_fusion.3
  87.4 4.0 %fusion.7 = f32[16,504]{1,0:T(8,128)} fusion(bf16[4096,504]{0,1:T(8,128)(2,1)} %param.14, bf16[16,1,4096]{2,1,0:T(2,128)(2,1)S(1)} %constant_dynamic-slice_fusion.3), kind=kOutput, calls=%fused_computation.11 | convolution fusion | flops 66060288 | bytes 4292096 | tf_op jit(solution)/shard_map/dot_general | solution.py:74
  91.4 0.0 reduce-scatter.2.cloned.1.call-update
  91.4 0.6 dynamic-slice
  92.7 4.2 %reduce-scatter.2.cloned.1.call-done = f32[8,504]{1,0:T(8,128)} async-done(((f32[16,504]{1,0:T(8,128)}), f32[8,504]{1,0:T(8,128)}) %reduce-scatter.2.cloned.1.call-update) | async-done | bytes 16144 | tf_op jit(solution)/shard_map/reduce_scatter | solution.py:75
  96.9 0.8 reduce_max.9
  97.7 0.2 dynamic-update-slice
  98.0 0.9 select_reduce_fusion
  98.9 0.2 dynamic-update-slice.2
  99.2 0.2 dynamic-update-slice.1
  99.4 21.5 %all-reduce.3 = (f32[64]{0:T(128)S(1)}, f32[64]{0:T(128)S(1)}, f32[64]{0:T(128)S(1)}) all-reduce(f32[64]{0:T(128)S(1)} %dynamic-update-slice, f32[64]{0:T(128)S(1)} %dynamic-update-slice.1, f32[64]{0:T(128)S(1)} %dynamic-update-slice.2), channel_id=2, replica_groups=mesh['groups'=2,'vocab'=8,'mp'=2] {'vocab'}, use_global_device_ids=true, to_apply=%add | all-reduce | flops 192 | bytes 1536
  120.9 0.1 reshape.19
  121.0 0.1 reshape.20
  121.1 0.1 reshape.21
  121.1 0.3 while.19
  121.4 0.5 log_subtract_fusion
  (20 shorter events, 0.3 us)
Async XLA Ops:
  6.5 84.9 %copy-start.3 = (u32[32]{0:T(128)S(1)}, u32[32]{0:T(128)}, u32[]{:S(2)}) copy-start(u32[32]{0:T(128)} %constant.71) | copy-start | bytes 388
  6.5 48.8 %copy-start.1 = (bf16[8192]{0:T(1024)(128)(2,1)S(1)}, bf16[8192]{0:T(1024)(128)(2,1)}, u32[]{:S(2)}) copy-start(bf16[8192]{0:T(1024)(128)(2,1)} %param.13) | copy-start | bytes 49156
  6.5 59.6 %copy-start = (bf16[1,8192]{1,0:T(2,128)(2,1)S(1)}, bf16[1,8192]{1,0:T(2,128)(2,1)}, u32[]{:S(2)}) copy-start(bf16[1,8192]{1,0:T(2,128)(2,1)} %param.12) | copy-start | bytes 49156
  6.5 84.8 %copy-start.2 = (s32[8]{0:T(128)S(1)}, s32[8]{0:T(128)}, u32[]{:S(2)}) copy-start(s32[8]{0:T(128)} %param.15) | copy-start | bytes 100
  49.7 12.4 %all-to-all-start = ((f32[8,2,1,1024]{3,1,2,0:T(2,128)}), f32[8,2,1,1024]{3,1,2,0:T(2,128)S(1)}, u32[]{:S(2)}, u32[]{:S(2)}) async-start(f32[8,2,1,1024]{3,1,2,0:T(2,128)} %bitcast.4), calls=%async_computation | async-start | bytes 131072 | tf_op jit(solution)/shard_map/all_to_all | solution.py:48
  55.2 41.7 %reduce-scatter.2.cloned.1.call-start = ((), (), s32[]{:S(2)}) async-start(), calls=%async_computation.3 | async-start | bytes 49152 | tf_op jit(solution)/shard_map/reduce_scatter | solution.py:75
Sparse Core Ops, SparseCore 0:
  91.5 5.3 reduce-scatter.1
